TPU v7x, 32 devices: a whole 2x2x4 slice. The times are simulated.
32 devices in a mesh: dp: 16 (over z, y, core), tensor: 2 (over x).
Axes of the slice: x: 2, y: 2, z: 4, core: 2. Of those that a mesh axis runs over, the one named last changes fastest.
Arguments:
- tokens: bfloat16 [4096, 1024], P(('dp', 'tensor')), may hold values from -6 to 6
- out_cotangent: bfloat16 [4096, 1024], P(('dp', 'tensor')), may hold values from -6 to 6
- seq_lengths: int32 [16], P('dp'), may hold values from 1 to 256, 2048 in all
- norm_gain1: float32 [1024], replicated, may hold values from 0.1 to 1.9
- query_weight: bfloat16 [1024, 1024], P('dp', 'tensor'), may hold values from -0.1875 to 0.1875
- key_weight: bfloat16 [1024, 1024], P('dp', 'tensor'), may hold values from -0.1875 to 0.1875
- value_weight: bfloat16 [1024, 2048], P('dp', 'tensor'), may hold values from -0.1875 to 0.1875
- out_gate_weight: bfloat16 [1024, 2048], P('dp', 'tensor'), may hold values from -0.1875 to 0.1875
- beta_weight: bfloat16 [1024, 8], P('dp', 'tensor'), may hold values from -0.1875 to 0.1875
- decay_weight: bfloat16 [1024, 8], P('dp', 'tensor'), may hold values from -0.1875 to 0.1875
- conv_query: float32 [4, 1024], P(None, 'tensor'), may hold values from -3 to 3
- conv_key: float32 [4, 1024], P(None, 'tensor'), may hold values from -3 to 3
- conv_value: float32 [4, 2048], P(None, 'tensor'), may hold values from -3 to 3
- decay_log_rate: float32 [8], P('tensor'), may hold values from -4 to 1
- decay_bias: float32 [8], P('tensor'), may hold values from -4 to 0
- out_gain: float32 [256], replicated, may hold values from 0.1 to 1.9
- out_weight: bfloat16 [1024, 2048], P('dp', 'tensor'), may hold values from -0.25 to 0.25
- norm_gain2: float32 [1024], replicated, may hold values from 0.1 to 1.9
- ffn_gate_weight: bfloat16 [1024, 2816], P('dp', 'tensor'), may hold values from -0.1875 to 0.1875
- ffn_up_weight: bfloat16 [1024, 2816], P('dp', 'tensor'), may hold values from -0.1875 to 0.1875
- ffn_down_weight: bfloat16 [1024, 2816], P('dp', 'tensor'), may hold values from -0.109375 to 0.109375
Outputs:
- output: bfloat16 [4096, 1024], P(('dp', 'tensor'))
- grad_tokens: bfloat16 [4096, 1024], P(('dp', 'tensor'))
- grad_norm_gain1: float32 [1024], replicated
- grad_query_weight: float32 [1024, 1024], P('dp', 'tensor')
- grad_key_weight: float32 [1024, 1024], P('dp', 'tensor')
- grad_value_weight: float32 [1024, 2048], P('dp', 'tensor')
- grad_out_gate_weight: float32 [1024, 2048], P('dp', 'tensor')
- grad_beta_weight: float32 [1024, 8], P('dp', 'tensor')
- grad_decay_weight: float32 [1024, 8], P('dp', 'tensor')
- grad_conv_query: float32 [4, 1024], replicated
- grad_conv_key: float32 [4, 1024], replicated
- grad_conv_value: float32 [4, 2048], replicated
- grad_decay_log_rate: float32 [8], replicated
- grad_decay_bias: float32 [8], replicated
- grad_out_gain: float32 [256], replicated
- grad_out_weight: float32 [1024, 2048], P('dp', 'tensor')
- grad_norm_gain2: float32 [1024], replicated
- grad_ffn_gate_weight: float32 [1024, 2816], P('dp', 'tensor')
- grad_ffn_up_weight: float32 [1024, 2816], P('dp', 'tensor')
- grad_ffn_down_weight: float32 [1024, 2816], P('dp', 'tensor')
Inputs may be any that keep to these rules, and one draw needn't show every extreme that they name: `seq_lengths`: the number of valid tokens of each sequence; the largest is exactly 256.
All inputs are finite; a program needn't handle non-finite values. No bound on the sum of `seq_lengths` on one device may be relied on, other than what follows from the above.
Results may differ from a plain program's by a relative error of at most 0.012.
Values may be sent and summed in bfloat16 or wider, within the bound.
No kernel may reach another device: no remote copies, remote signals or barrier semaphores. Data moves between devices by JAX's collectives and lax.ppermute only.
A program may use at most 192 MiB of HBM per device.

v0:
```python
import jax
import jax.numpy as jnp
from jax import lax
from jax.sharding import PartitionSpec as P

GROUP = 64
highest = lax.Precision.HIGHEST


def plain_dot(left, right):
    return jnp.dot(left, right, preferred_element_type=jnp.float32)


def left_dot(left, right):
    return lax.dot_general(
        left, right, (((0,), (0,)), ((), ())), preferred_element_type=jnp.float32
    )


def right_dot(left, right):
    return lax.dot_general(
        left, right, (((1,), (1,)), ((), ())), preferred_element_type=jnp.float32
    )


def exact_dot(left, right):
    return jnp.dot(left, right, precision=highest)


def rms_rows(inputs, gain):
    wide_rows = inputs.astype(jnp.float32)
    inverse = lax.rsqrt(jnp.mean(wide_rows * wide_rows, -1, keepdims=True) + 1e-05)
    normed = wide_rows * inverse
    return (normed, inverse, (normed * gain).astype(jnp.bfloat16))


def rms_back(grad_rows, normed, inverse, gain):
    scaled = grad_rows * gain
    grad_in = inverse * (scaled - normed * jnp.mean(scaled * normed, -1, keepdims=True))
    return (grad_in, jnp.sum(grad_rows * normed, 0))


def causal_conv(projected, kernel):
    kernel_len = kernel.shape[0]
    summed = kernel[kernel_len - 1] * projected
    for offset in range(1, kernel_len):
        shifted = jnp.pad(projected[:-offset], ((offset, 0), (0, 0)))
        summed = summed + kernel[kernel_len - 1 - offset] * shifted
    return summed


def delta_block(state, element):
    block_query, block_key, block_value, block_beta, block_gate = element
    block_len = block_key.shape[0]
    value_dim = block_value.shape[1]
    lower_all = jnp.tril(jnp.ones((block_len, block_len), dtype=bool))
    strict_lower = jnp.tril(jnp.ones((block_len, block_len), dtype=bool), -1)
    cumulative = jnp.cumsum(block_gate)
    spread = cumulative[:, None] - cumulative[None, :]
    decays = jnp.where(lower_all, jnp.exp(jnp.where(lower_all, spread, 0.0)), 0.0)
    key_key = exact_dot(block_key, block_key.T)
    coupling = jnp.where(strict_lower, block_beta[:, None] * key_key * decays, 0.0)
    stacked = jnp.concatenate(
        [
            block_beta[:, None] * block_value,
            (block_beta * jnp.exp(cumulative))[:, None] * block_key,
        ],
        axis=1,
    )
    solved = lax.linalg.triangular_solve(
        coupling + jnp.eye(block_len, dtype=jnp.float32),
        stacked,
        left_side=True,
        lower=True,
        unit_diagonal=True,
    )
    updates = solved[:, :value_dim] - exact_dot(solved[:, value_dim:], state.T)
    query_key = jnp.where(lower_all, exact_dot(block_query, block_key.T) * decays, 0.0)
    outputs = jnp.exp(cumulative)[:, None] * exact_dot(block_query, state.T) + exact_dot(
        query_key, updates
    )
    final_log = cumulative[-1]
    new_state = jnp.exp(final_log) * state + exact_dot(
        updates.T, block_key * jnp.exp(final_log - cumulative)[:, None]
    )
    return (new_state, outputs)


def delta_rule(query_rows, key_rows, value_rows, beta_rows, log_gates, block_len):
    length, head_count, key_dim = key_rows.shape
    value_dim = value_rows.shape[2]
    blocks = length // block_len

    def split_heads(array):
        shaped = array.reshape((blocks, block_len) + array.shape[1:])
        return jnp.moveaxis(shaped, 2, 0)

    def one_head(head_query, head_key, head_value, head_beta, head_gate):
        start_state = jnp.zeros((value_dim, key_dim), jnp.float32)
        unused, outputs = lax.scan(
            delta_block, start_state, (head_query, head_key, head_value, head_beta, head_gate)
        )
        return outputs

    per_head = jax.vmap(one_head)(
        split_heads(query_rows),
        split_heads(key_rows),
        split_heads(value_rows),
        split_heads(beta_rows),
        split_heads(log_gates),
    )
    return jnp.transpose(per_head, (1, 2, 0, 3)).reshape(length, head_count, value_dim)


def mixer(
    proj_query,
    proj_key,
    proj_value,
    proj_gate,
    proj_beta,
    proj_decay,
    conv_query,
    conv_key,
    conv_value,
    decay_log_rate,
    decay_bias,
    out_gain,
):
    length = proj_query.shape[0]
    head_count = proj_beta.shape[1]
    query_rows = jax.nn.silu(causal_conv(proj_query, conv_query)).reshape(length, head_count, -1)
    key_rows = jax.nn.silu(causal_conv(proj_key, conv_key)).reshape(length, head_count, -1)
    value_rows = jax.nn.silu(causal_conv(proj_value, conv_value)).reshape(length, head_count, -1)
    key_dim = query_rows.shape[2]
    query_rows = (
        query_rows
        * lax.rsqrt(jnp.sum(query_rows * query_rows, -1, keepdims=True) + 1e-06)
        * key_dim ** (-0.5)
    )
    key_rows = key_rows * lax.rsqrt(jnp.sum(key_rows * key_rows, -1, keepdims=True) + 1e-06)
    beta_rows = jax.nn.sigmoid(proj_beta)
    log_gates = -jnp.exp(decay_log_rate) * jax.nn.softplus(proj_decay + decay_bias)
    mixed = delta_rule(query_rows, key_rows, value_rows, beta_rows, log_gates, GROUP)
    inverse = lax.rsqrt(jnp.mean(mixed * mixed, -1, keepdims=True) + 1e-05)
    gated = mixed * inverse * out_gain * jax.nn.silu(proj_gate.reshape(length, head_count, -1))
    return gated.reshape(length, -1)


def split_columns(array, widths):
    pieces = []
    offset = 0
    for width in widths:
        pieces.append(array[:, offset : offset + width])
        offset = offset + width
    return pieces


def on_device(
    tokens,
    out_cotangent,
    seq_lengths,
    norm_gain1,
    query_weight,
    key_weight,
    value_weight,
    out_gate_weight,
    beta_weight,
    decay_weight,
    conv_query,
    conv_key,
    conv_value,
    decay_log_rate,
    decay_bias,
    out_gain,
    out_weight,
    norm_gain2,
    ffn_gate_weight,
    ffn_up_weight,
    ffn_down_weight,
):
    local_rows = tokens.shape[0]
    tensor_index = lax.axis_index("tensor")
    tensor_count = lax.axis_size("tensor")
    seq_length = seq_lengths[0]
    local_pos = tensor_index * local_rows + jnp.arange(local_rows, dtype=jnp.int32)
    local_mask = (local_pos < seq_length).astype(jnp.float32)[:, None]
    whole_mask = (jnp.arange(local_rows * tensor_count, dtype=jnp.int32) < seq_length).astype(
        jnp.bfloat16
    )[:, None]
    key_cols = query_weight.shape[1]
    value_cols = value_weight.shape[1]
    head_cols = beta_weight.shape[1]
    hidden_cols = ffn_gate_weight.shape[1]
    mixer_widths = [key_cols, key_cols, value_cols, value_cols, head_cols, head_cols]
    mixer_joined = jnp.concatenate(
        [query_weight, key_weight, value_weight, out_gate_weight, beta_weight, decay_weight], axis=1
    )
    ffn_joined = jnp.concatenate([ffn_gate_weight, ffn_up_weight], axis=1)
    normed1, inverse1, hidden1 = rms_rows(tokens, norm_gain1)
    whole1 = lax.all_gather(hidden1, "tensor", axis=0, tiled=True)
    mixer_full = (
        lax.all_gather(mixer_joined, "dp", axis=0, tiled=True),
        lax.all_gather(out_weight, "dp", axis=0, tiled=True),
    )
    projections = split_columns(plain_dot(whole1, mixer_full[0]), mixer_widths)
    mixed_out, pullback = jax.vjp(
        mixer,
        projections[0],
        projections[1],
        projections[2],
        projections[3],
        projections[4],
        projections[5],
        conv_query,
        conv_key,
        conv_value,
        decay_log_rate,
        decay_bias,
        out_gain,
    )
    mixed_half = mixed_out.astype(jnp.bfloat16)
    out_full = mixer_full[1]
    branch = lax.psum_scatter(
        right_dot(mixed_half, out_full), "tensor", scatter_dimension=0, tiled=True
    )
    residual = tokens.astype(jnp.float32) + branch
    normed2, inverse2, hidden2 = rms_rows(residual, norm_gain2)
    whole2 = lax.all_gather(hidden2, "tensor", axis=0, tiled=True)
    ffn_full = (
        lax.all_gather(ffn_joined, "dp", axis=0, tiled=True),
        lax.all_gather(ffn_down_weight, "dp", axis=0, tiled=True),
    )
    pre_both = plain_dot(whole2, ffn_full[0])
    gate_pre = pre_both[:, :hidden_cols]
    up_pre = pre_both[:, hidden_cols:]
    gate_act = jax.nn.silu(gate_pre)
    inner_act = (gate_act * up_pre).astype(jnp.bfloat16)
    down_full = ffn_full[1]
    ffn_branch = lax.psum_scatter(
        right_dot(inner_act, down_full).astype(jnp.bfloat16),
        "tensor",
        scatter_dimension=0,
        tiled=True,
    ).astype(jnp.float32)
    output = (local_mask * (residual + ffn_branch)).astype(jnp.bfloat16)
    grad_whole = lax.all_gather(out_cotangent, "tensor", axis=0, tiled=True) * whole_mask
    grad_inner = plain_dot(grad_whole, ffn_full[1])
    sigma_gate = jax.nn.sigmoid(gate_pre)
    grad_gate_pre = (
        grad_inner * up_pre * sigma_gate * (1.0 + gate_pre * (1.0 - sigma_gate))
    ).astype(jnp.bfloat16)
    grad_up_pre = (grad_inner * gate_act).astype(jnp.bfloat16)
    grad_pre_both = jnp.concatenate([grad_gate_pre, grad_up_pre], axis=1)
    grad_hidden2 = lax.psum_scatter(
        right_dot(grad_pre_both, ffn_full[0]), "tensor", scatter_dimension=0, tiled=True
    )
    grad_normed2, second_gain_gradient = rms_back(grad_hidden2, normed2, inverse2, norm_gain2)
    grad_residual = local_mask * out_cotangent.astype(jnp.float32) + grad_normed2
    gate_up_part = left_dot(whole2, grad_pre_both)
    down_part = left_dot(grad_whole, inner_act)
    ffn_shard = lax.psum_scatter(
        jnp.concatenate([gate_up_part, down_part], axis=1), "dp", scatter_dimension=0, tiled=True
    )
    grad_whole1 = lax.all_gather(grad_residual.astype(jnp.bfloat16), "tensor", axis=0, tiled=True)
    grad_mixed = plain_dot(grad_whole1, mixer_full[1])
    mixer_gradient_list = pullback(grad_mixed)
    grad_projs = jnp.concatenate(
        [member.astype(jnp.bfloat16) for member in mixer_gradient_list[:6]], axis=1
    )
    grad_hidden1 = lax.psum_scatter(
        right_dot(grad_projs, mixer_full[0]).astype(jnp.bfloat16),
        "tensor",
        scatter_dimension=0,
        tiled=True,
    ).astype(jnp.float32)
    grad_normed1, first_gain_gradient = rms_back(grad_hidden1, normed1, inverse1, norm_gain1)
    grad_tokens = (grad_residual + grad_normed1).astype(jnp.bfloat16)
    proj_part = left_dot(whole1, grad_projs)
    out_part = left_dot(grad_whole1, mixed_half)
    mixer_shard = lax.psum_scatter(
        jnp.concatenate([proj_part, out_part], axis=1), "dp", scatter_dimension=0, tiled=True
    )
    mixer_grads = split_columns(mixer_shard, mixer_widths + [value_cols])
    ffn_grads = split_columns(ffn_shard, [hidden_cols, hidden_cols, hidden_cols])

    def widen(element, axis_pos):
        size_one = element.shape[axis_pos]
        shape_all = list(element.shape)
        shape_all[axis_pos] = size_one * tensor_count
        return lax.dynamic_update_slice_in_dim(
            jnp.zeros(shape_all, jnp.float32), element, tensor_index * size_one, axis_pos
        )

    small_sums = lax.psum(
        (
            first_gain_gradient,
            second_gain_gradient,
            mixer_gradient_list[11],
            widen(mixer_gradient_list[6], 1),
            widen(mixer_gradient_list[7], 1),
            widen(mixer_gradient_list[8], 1),
            widen(mixer_gradient_list[9], 0),
            widen(mixer_gradient_list[10], 0),
        ),
        ("dp", "tensor"),
    )
    return (
        output,
        grad_tokens,
        small_sums[0],
        mixer_grads[0],
        mixer_grads[1],
        mixer_grads[2],
        mixer_grads[3],
        mixer_grads[4],
        mixer_grads[5],
        small_sums[3],
        small_sums[4],
        small_sums[5],
        small_sums[6],
        small_sums[7],
        small_sums[2],
        mixer_grads[6],
        small_sums[1],
        ffn_grads[0],
        ffn_grads[1],
        ffn_grads[2],
    )


def solution(mesh):
    in_specs = (
        P(("dp", "tensor"), None),
        P(("dp", "tensor"), None),
        P("dp"),
        P(),
        P("dp", "tensor"),
        P("dp", "tensor"),
        P("dp", "tensor"),
        P("dp", "tensor"),
        P("dp", "tensor"),
        P("dp", "tensor"),
        P(None, "tensor"),
        P(None, "tensor"),
        P(None, "tensor"),
        P("tensor"),
        P("tensor"),
        P(),
        P("dp", "tensor"),
        P(),
        P("dp", "tensor"),
        P("dp", "tensor"),
        P("dp", "tensor"),
    )
    out_specs = (
        P(("dp", "tensor"), None),
        P(("dp", "tensor"), None),
        P(),
        P("dp", "tensor"),
        P("dp", "tensor"),
        P("dp", "tensor"),
        P("dp", "tensor"),
        P("dp", "tensor"),
        P("dp", "tensor"),
        P(),
        P(),
        P(),
        P(),
        P(),
        P(),
        P("dp", "tensor"),
        P(),
        P("dp", "tensor"),
        P("dp", "tensor"),
        P("dp", "tensor"),
    )
    return jax.shard_map(
        on_device, mesh=mesh, in_specs=in_specs, out_specs=out_specs, check_vma=False
    )
```

profile of v0, /device:TPU:8, one launch (start us, length us, event | category | flops | bytes accessed | tf_op | source)
XLA Modules:
  0.0 1243.3 jit_solution(5438580144339664088)
XLA Ops:
  14.0 8.7 all_gather.24
  23.0 52.0 %all-gather.5.cloned.1.call-done = bf16[1024,3080]{1,0:T(8,128)(2,1)} async-done(((bf16[64,3080]{1,0:T(8,128)(2,1)}), bf16[1024,3080]{1,0:T(8,128)(2,1)}) %all-gather.5.cloned.1.call-update) | async-done | bytes 6307856 | tf_op jit(solution)/shard_map/all_gather | solution.py:202
  75.0 5.6 fusion.229
  109.3 144.0 %while.98 = (s32[]{:T(128)}, f32[4,256,128]{2,1,0:T(8,128)S(1)}, f32[4,4,64,256]{3,1,2,0:T(4,128)}, f32[4,4,64,64]{3,2,1,0:T(8,128)}, f32[4,4,128,64]{2,3,1,0:T(...) while((s32[]{:T(128)}, f32[4,256,128]{2,1,0:T(8,128)S(1)}, ...), condition=%wide.region_5.6_spmd.clone.clone, body=%wide.region_3.5_spmd.clone.clone.sunk | while | flops 479990848 | bytes 12846126 | solution.py:100
  114.7 19.7 %custom-call.48 = f32[4,1,64,64]{2,3,1,0:T(8,128)S(1)} custom-call(f32[4,1,64,64]{3,2,1,0:T(8,128)S(1)} %add_bitcast_fusion.4), custom_call_target="InvertDiagBlocksLowerTriangular" | custom-call | tf_op jit(solution)/shard_map/jvp(vmap())/while/body/eval_jaxpr/triangular_solve | solution.py:70
  150.6 19.7 %custom-call.48 = f32[4,1,64,64]{2,3,1,0:T(8,128)S(1)} custom-call(f32[4,1,64,64]{3,2,1,0:T(8,128)S(1)} %add_bitcast_fusion.4), custom_call_target="InvertDiagBlocksLowerTriangular" | custom-call | tf_op jit(solution)/shard_map/jvp(vmap())/while/body/eval_jaxpr/triangular_solve | solution.py:70
  186.6 19.7 %custom-call.48 = f32[4,1,64,64]{2,3,1,0:T(8,128)S(1)} custom-call(f32[4,1,64,64]{3,2,1,0:T(8,128)S(1)} %add_bitcast_fusion.4), custom_call_target="InvertDiagBlocksLowerTriangular" | custom-call | tf_op jit(solution)/shard_map/jvp(vmap())/while/body/eval_jaxpr/triangular_solve | solution.py:70
  222.5 19.7 %custom-call.48 = f32[4,1,64,64]{2,3,1,0:T(8,128)S(1)} custom-call(f32[4,1,64,64]{3,2,1,0:T(8,128)S(1)} %add_bitcast_fusion.4), custom_call_target="InvertDiagBlocksLowerTriangular" | custom-call | tf_op jit(solution)/shard_map/jvp(vmap())/while/body/eval_jaxpr/triangular_solve | solution.py:70
  267.8 14.3 %all_gather.30 = bf16[256,1024]{1,0:T(8,128)(2,1)S(1)} all-gather(bf16[128,1024]{1,0:T(8,128)(2,1)S(1)} %copy-done.41), channel_id=1, replica_groups=mesh['dp'=16,'tensor'=2] {'tensor'}, dimensions={0}, use_global_device_ids=true | all-gather | bytes 786432 | tf_op jit(solution)/shard_map/all_gather | solution.py:246
  282.1 7.2 reduce-scatter.9.cloned.1.call-done
  290.7 8.8 all_gather.27
  299.5 50.0 %all-gather.9.cloned.1.call-done = bf16[1024,2816]{1,0:T(8,128)(2,1)} async-done(((bf16[64,2816]{1,0:T(8,128)(2,1)}), bf16[1024,2816]{1,0:T(8,128)(2,1)}) %all-gather.9.cloned.1.call-update) | async-done | bytes 5767184 | tf_op jit(solution)/shard_map/all_gather | solution.py:230
  349.5 5.9 fusion.231
  355.4 38.8 %all-gather.11.cloned.1.call-done = bf16[1024,1408]{1,0:T(8,128)(2,1)} async-done(((bf16[64,1408]{1,0:T(8,128)(2,1)}), bf16[1024,1408]{1,0:T(8,128)(2,1)}) %all-gather.11.cloned.1.call-update) | async-done | bytes 2883600 | tf_op jit(solution)/shard_map/all_gather | solution.py:231
  394.3 5.0 multiply_convert_fusion.1
  415.9 4.8 fusion.191
  420.8 5.9 fusion.169
  428.6 10.6 reduce-scatter.11.cloned.1.call-done
  441.7 8.9 all_gather.31
  464.9 191.4 %while.99 = (s32[]{:T(128)}, f32[4,256,128]{2,1,0:T(8,128)S(1)}, f32[4,4,64,128]{3,2,1,0:T(8,128)}, f32[4,4,64,128]{3,2,1,0:T(8,128)}, f32[4,4,64,256]{3,2,1,0:T...) while((s32[]{:T(128)}, f32[4,256,128]{2,1,0:T(8,128)S(1)}, ...), condition=%wide.region_24.25_spmd.clone.clone, body=%wide.region_13.24_spmd.clone.clone.sunk | while | flops 971683904 | bytes 18991880 | solution.py:100
  472.6 19.7 %custom-call.49 = f32[4,1,64,64]{2,3,1,0:T(8,128)S(1)} custom-call(f32[4,1,64,64]{3,2,1,0:T(8,128)S(1)} %add_bitcast_fusion.5), custom_call_target="InvertDiagBlocksLowerTriangular" | custom-call | tf_op jit(solution)/shard_map/transpose(jvp(vmap()))/while/body/eval_jaxpr/triangular_solve | solution.py:70
  520.4 19.7 %custom-call.49 = f32[4,1,64,64]{2,3,1,0:T(8,128)S(1)} custom-call(f32[4,1,64,64]{3,2,1,0:T(8,128)S(1)} %add_bitcast_fusion.5), custom_call_target="InvertDiagBlocksLowerTriangular" | custom-call | tf_op jit(solution)/shard_map/transpose(jvp(vmap()))/while/body/eval_jaxpr/triangular_solve | solution.py:70
  568.2 19.7 %custom-call.49 = f32[4,1,64,64]{2,3,1,0:T(8,128)S(1)} custom-call(f32[4,1,64,64]{3,2,1,0:T(8,128)S(1)} %add_bitcast_fusion.5), custom_call_target="InvertDiagBlocksLowerTriangular" | custom-call | tf_op jit(solution)/shard_map/transpose(jvp(vmap()))/while/body/eval_jaxpr/triangular_solve | solution.py:70
  616.0 19.7 %custom-call.49 = f32[4,1,64,64]{2,3,1,0:T(8,128)S(1)} custom-call(f32[4,1,64,64]{3,2,1,0:T(8,128)S(1)} %add_bitcast_fusion.5), custom_call_target="InvertDiagBlocksLowerTriangular" | custom-call | tf_op jit(solution)/shard_map/transpose(jvp(vmap()))/while/body/eval_jaxpr/triangular_solve | solution.py:70
  682.8 4.9 multiply_reduce_fusion.3
  701.1 5.6 convolution_convert_fusion
  706.8 11.9 pad_maximum_fusion
  722.5 7.2 pad_maximum_fusion.1
  729.6 19.0 %copy.246 = f32[1024,4104]{1,0:T(8,128)} copy(f32[1024,4104]{0,1:T(8,128)} %pad_maximum_fusion.1) | data formatting | bytes 33619968
  753.3 153.3 %reduce-scatter.17.cloned.1.call-done = f32[64,4224]{1,0:T(8,128)} async-done(((f32[1024,4224]{1,0:T(8,128)}), f32[64,4224]{1,0:T(8,128)}) %reduce-scatter.17.cloned.1.call-update) | async-done | bytes 1081360 | tf_op jit(solution)/shard_map/reduce_scatter | solution.py:261
  908.8 182.9 %reduce-scatter.19.cloned.1.call-done = f32[64,4104]{1,0:T(8,128)} async-done(((f32[1024,4104]{1,0:T(8,128)}), f32[64,4104]{1,0:T(8,128)}) %reduce-scatter.19.cloned.1.call-update) | async-done | bytes 1050640
  1097.7 128.7 %all-reduce.36.cloned.1.call-done = (f32[1024]{0:T(1024)}, f32[4,1024]{1,0:T(4,128)}, f32[4,1024]{1,0:T(4,128)}, f32[4,2048]{1,0:T(4,128)}, f32[8]{0:T(128)}, /*index=5*/f32[8]{0:T(128)}, f32[256]{0:T(256)}, f32[1024]{0:T(1024)}) async-done(((f32[1024]{0:T(1024)}, f32[4,1024]{1,0:T(4,128)}, f32[4,1024]{1,0:T(4,128)}, f32[4,2048]{1,0:T(4,128)}, f32[8]{0:T(128)}, /*index=5*/f32[8]{0:T(128)}, f32[256]{0:T(256)}, ...) | async-done | bytes 74832 | tf_op jit(solution)/shard_map/psum | solution.py:294
  (703 shorter events, 328.1 us)
Async XLA Ops:
  7.2 67.7 %all-gather.5.cloned.1.call-start = ((), (), s32[]{:S(2)}) async-start(), calls=%async_computation.6 | async-start | bytes 6963200 | tf_op jit(solution)/shard_map/all_gather | solution.py:202
  10.8 251.2 %all-gather.7.cloned.1.call-start = ((), (), s32[]{:S(2)}) async-start(), calls=%async_computation.7 | async-start | bytes 2228224 | tf_op jit(solution)/shard_map/all_gather | solution.py:203
  11.5 277.8 %reduce-scatter.9.cloned.1.call-start = ((), (), s32[]{:S(2)}) async-start(), calls=%async_computation.8 | async-start | bytes 1572864 | tf_op jit(solution)/shard_map/reduce_scatter | solution.py:223
  12.9 67.7 %copy-start.105 = (f32[128]{0:T(128)}, f32[128]{0:T(128)S(1)}, u32[]{:S(2)}) copy-start(f32[128]{0:T(128)S(1)} %add_rsqrt_fusion.3) | copy-start | bytes 1540
  22.7 52.3 %copy-start.31 = (bf16[256,1024]{1,0:T(8,128)(2,1)}, bf16[256,1024]{1,0:T(8,128)(2,1)S(1)}, u32[]{:S(2)}) copy-start(bf16[256,1024]{1,0:T(8,128)(2,1)S(1)} %all_gather.24) | copy-start | bytes 1572868
  22.7 236.4 %copy-start.67 = (f32[1,2,4,128]{3,1,2,0:T(2,128)}, f32[1,2,4,128]{3,1,2,0:T(2,128)S(1)}, u32[]{:S(2)}) copy-start(f32[1,2,4,128]{3,1,2,0:T(2,128)S(1)} %copy.322) | copy-start | bytes 12292
  22.7 62.8 %copy-start.111 = (f32[4]{0:T(128)}, f32[4]{0:T(128)S(1)}, u32[]{:S(2)}) copy-start(f32[4]{0:T(128)S(1)} %exponential_negate_fusion) | copy-start | bytes 52
  22.8 63.0 %copy-start.85 = (f32[1,512]{1,0:T(1,128)}, f32[1,512]{1,0:T(1,128)S(1)}, u32[]{:S(2)}) copy-start(f32[1,512]{1,0:T(1,128)S(1)} %get-tuple-element.2632) | copy-start | bytes 6148
  22.8 63.0 %copy-start.89 = (f32[1,512]{1,0:T(1,128)}, f32[1,512]{1,0:T(1,128)S(1)}, u32[]{:S(2)}) copy-start(f32[1,512]{1,0:T(1,128)S(1)} %get-tuple-element.2633) | copy-start | bytes 6148
  22.8 63.0 %copy-start.93 = (f32[1,512]{1,0:T(1,128)}, f32[1,512]{1,0:T(1,128)S(1)}, u32[]{:S(2)}) copy-start(f32[1,512]{1,0:T(1,128)S(1)} %get-tuple-element.2631) | copy-start | bytes 6148
  22.8 63.0 %copy-start.97 = (f32[1,512]{1,0:T(1,128)}, f32[1,512]{1,0:T(1,128)S(1)}, u32[]{:S(2)}) copy-start(f32[1,512]{1,0:T(1,128)S(1)} %get-tuple-element.2630) | copy-start | bytes 6148
  22.8 63.0 %copy-start.83 = (f32[1,512]{1,0:T(1,128)}, f32[1,512]{1,0:T(1,128)S(1)}, u32[]{:S(2)}) copy-start(f32[1,512]{1,0:T(1,128)S(1)} %get-tuple-element.2636) | copy-start | bytes 6148
  22.8 63.0 %copy-start.87 = (f32[1,512]{1,0:T(1,128)}, f32[1,512]{1,0:T(1,128)S(1)}, u32[]{:S(2)}) copy-start(f32[1,512]{1,0:T(1,128)S(1)} %get-tuple-element.2637) | copy-start | bytes 6148
  22.8 63.0 %copy-start.91 = (f32[1,512]{1,0:T(1,128)}, f32[1,512]{1,0:T(1,128)S(1)}, u32[]{:S(2)}) copy-start(f32[1,512]{1,0:T(1,128)S(1)} %get-tuple-element.2635) | copy-start | bytes 6148
  22.9 63.0 %copy-start.95 = (f32[1,512]{1,0:T(1,128)}, f32[1,512]{1,0:T(1,128)S(1)}, u32[]{:S(2)}) copy-start(f32[1,512]{1,0:T(1,128)S(1)} %get-tuple-element.2634) | copy-start | bytes 6148
  22.9 72.0 %copy-start.69 = (f32[1,1024]{1,0:T(1,128)}, f32[1,1024]{1,0:T(1,128)S(1)}, u32[]{:S(2)}) copy-start(f32[1,1024]{1,0:T(1,128)S(1)} %get-tuple-element.2628) | copy-start | bytes 12292
  22.9 72.0 %copy-start.71 = (f32[1,1024]{1,0:T(1,128)}, f32[1,1024]{1,0:T(1,128)S(1)}, u32[]{:S(2)}) copy-start(f32[1,1024]{1,0:T(1,128)S(1)} %get-tuple-element.2629) | copy-start | bytes 12292
  22.9 72.0 %copy-start.73 = (f32[1,1024]{1,0:T(1,128)}, f32[1,1024]{1,0:T(1,128)S(1)}, u32[]{:S(2)}) copy-start(f32[1,1024]{1,0:T(1,128)S(1)} %get-tuple-element.2627) | copy-start | bytes 12292
  22.9 72.0 %copy-start.81 = (f32[1,1024]{1,0:T(1,128)}, f32[1,1024]{1,0:T(1,128)S(1)}, u32[]{:S(2)}) copy-start(f32[1,1024]{1,0:T(1,128)S(1)} %get-tuple-element.2626) | copy-start | bytes 12292
  265.6 25.0 %copy-start.62 = (f32[1024]{0:T(1024)S(1)}, f32[1024]{0:T(1024)}, u32[]{:S(2)}) copy-start(f32[1024]{0:T(1024)} %param.42) | copy-start | bytes 12292
  265.6 83.9 %all-gather.9.cloned.1.call-start = ((), (), s32[]{:S(2)}) async-start(), calls=%async_computation.9 | async-start | bytes 6127616 | tf_op jit(solution)/shard_map/all_gather | solution.py:230
  266.5 127.8 %all-gather.11.cloned.1.call-start = ((), (), s32[]{:S(2)}) async-start(), calls=%async_computation.10 | async-start | bytes 3063808 | tf_op jit(solution)/shard_map/all_gather | solution.py:231
  267.0 159.7 %reduce-scatter.13.cloned.1.call-start = ((), (), s32[]{:S(2)}) async-start(), calls=%async_computation.12 | async-start | bytes 1572864 | tf_op jit(solution)/shard_map/reduce_scatter | solution.py:254
  267.8 126.5 %copy-start.113 = (bf16[256]{0:T(256)(128)(2,1)}, bf16[256]{0:T(256)(128)(2,1)S(1)}, u32[]{:S(2)}) copy-start(bf16[256]{0:T(256)(128)(2,1)S(1)} %compare_convert_fusion) | copy-start | bytes 1540
  282.1 112.1 %copy-start.29 = (bf16[256,1024]{1,0:T(8,128)(2,1)}, bf16[256,1024]{1,0:T(8,128)(2,1)S(1)}, u32[]{:S(2)}) copy-start(bf16[256,1024]{1,0:T(8,128)(2,1)S(1)} %all_gather.30) | copy-start | bytes 1572868
  290.6 64.8 %copy-start.107 = (f32[128]{0:T(128)}, f32[128]{0:T(128)S(1)}, u32[]{:S(2)}) copy-start(f32[128]{0:T(128)S(1)} %add_rsqrt_fusion.2) | copy-start | bytes 1540
  299.5 55.9 %copy-start.33 = (bf16[256,1024]{1,0:T(8,128)(2,1)}, bf16[256,1024]{1,0:T(8,128)(2,1)S(1)}, u32[]{:S(2)}) copy-start(bf16[256,1024]{1,0:T(8,128)(2,1)S(1)} %all_gather.27) | copy-start | bytes 1572868
  403.2 36.1 %reduce-scatter.11.cloned.1.call-start = ((), (), s32[]{:S(2)}) async-start(), calls=%async_computation.11 | async-start | bytes 786432 | tf_op jit(solution)/shard_map/reduce_scatter | solution.py:239
  415.8 333.5 %reduce-scatter.15.cloned.1.call-start = ((), (), s32[]{:S(2)}) async-start(), calls=%async_computation.13 | async-start | bytes 786432 | tf_op jit(solution)/shard_map/reduce_scatter | solution.py:270
  706.7 199.9 %reduce-scatter.17.cloned.1.call-start = ((), (), s32[]{:S(2)}) async-start(), calls=%async_computation.14 | async-start | bytes 18382848 | tf_op jit(solution)/shard_map/reduce_scatter | solution.py:261
  718.8 373.0 %reduce-scatter.19.cloned.1.call-start = ((), (), s32[]{:S(2)}) async-start(), calls=%async_computation.15 | async-start | bytes 18382848
  748.6 477.7 %all-reduce.36.cloned.1.call-start = ((), (), s32[]{:S(2)}) async-start(), calls=%async_computation.16 | async-start | bytes 151552 | tf_op jit(solution)/shard_map/psum | solution.py:294
  (102 other events, 509.5 us)
Sparse Core Ops, SparseCore 0:
  10.9 64.0 all-gather.4
  77.1 39.0 all-gather.6
  265.7 23.5 reduce-scatter.8
  292.1 57.4 all-gather.8
  351.6 42.5 all-gather.10
  403.3 18.9 reduce-scatter.12
  424.6 14.6 reduce-scatter.10
  706.9 14.6 reduce-scatter.14
  725.6 180.9 reduce-scatter.16
  910.6 181.0 reduce-scatter.18
  1099.9 126.4 all-reduce.35
where the time goes:
time: 1250 us; the launch traced here: 1240 us
  waiting for transfers between devices  625 us (50%)
  other arithmetic  276 us (22%)
  matrix products  149 us (12%)
  local copies, waits for them, and re-layouts  134 us (11%)
  blocking collectives  40.8 us (3%)
  between operations  16.3 us (1%)
    unnamed x12, waiting for transfers between devices  184 us
    another operation x40, other arithmetic, delta_block(): lax.linalg.triangular_solve(coupling + jnp.eye(block_len, dtype=jnp.float...  162 us
    reduce_scatter x1, waiting for transfers between devices, on_device(): lax.psum_scatter(jnp.concatenate([gate_up_part, down_part], axis=1), 'dp'...  153 us
    psum x1, waiting for transfers between devices, on_device(): lax.psum((first_gain_gradient, second_gain_gradient, mixer_gradient_list[...  129 us
    dot_general x72, matrix products, exact_dot(): return jnp.dot(left, right, precision=highest)  82 us
    all_gather x1, waiting for transfers between devices, on_device(): lax.all_gather(mixer_joined, 'dp', axis=0, tiled=True)  52 us
    all_gather x1, waiting for transfers between devices, on_device(): lax.all_gather(ffn_joined, 'dp', axis=0, tiled=True)  50 us
    unnamed x256, local copies, waits for them, and re-layouts  41.7 us
  transfers between devices with their start and end apart: 11, of which 8 were waited for; matrix products, arithmetic and copies ran while one was open for 22% of the time, Pallas kernels for 0%

commit v1 on v0

--- a/solution.py
+++ b/solution.py
@@ -291,19 +291,17 @@
             jnp.zeros(shape_all, jnp.float32), element, tensor_index * size_one, axis_pos
         )
 
-    small_sums = lax.psum(
-        (
-            first_gain_gradient,
-            second_gain_gradient,
-            mixer_gradient_list[11],
-            widen(mixer_gradient_list[6], 1),
-            widen(mixer_gradient_list[7], 1),
-            widen(mixer_gradient_list[8], 1),
-            widen(mixer_gradient_list[9], 0),
-            widen(mixer_gradient_list[10], 0),
-        ),
-        ("dp", "tensor"),
-    )
+    here_x = (
+        first_gain_gradient,
+        second_gain_gradient,
+        mixer_gradient_list[11],
+        widen(mixer_gradient_list[6], 1),
+        widen(mixer_gradient_list[7], 1),
+        widen(mixer_gradient_list[8], 1),
+        widen(mixer_gradient_list[9], 0),
+        widen(mixer_gradient_list[10], 0),
+    )
+    small_sums = lax.psum(lax.psum(here_x, axis_name="tensor"), "dp")
     return (
         output,
         grad_tokens,

time: 1250 us -> 1240 us (level)
  waiting for transfers between devices: 625 us -> 612 us
    psum x1 -> x2, waiting for transfers between devices: 129 us -> 89 us  [on_device(): small_sums = lax.psum(lax.psum(here_x, axis_name='tensor'), 'dp')]
    reduce_scatter x1, waiting for transfers between devices: 153 us -> 166 us  [on_device(): lax.psum_scatter(jnp.concatenate([gate_up_part, down_part], axis=1), 'dp'...]
    unnamed x12 -> x13, waiting for transfers between devices: 184 us -> 184 us
    unnamed x256 -> x254, local copies, waits for them, and re-layouts: 41.7 us -> 41.7 us
  transfers between devices with their start and end apart: 11 -> 12, of which waited for: 8 -> 10; matrix products, arithmetic and copies ran while one was open for 22% -> 22% of each run, Pallas kernels for 0% -> 0%
where the time goes in v1:
time: 1240 us; the launch traced here: 1230 us
  waiting for transfers between devices  612 us (49%)
  other arithmetic  276 us (22%)
  matrix products  150 us (12%)
  local copies, waits for them, and re-layouts  134 us (11%)
  blocking collectives  40.2 us (3%)
  between operations  16.6 us (1%)
    unnamed x13, waiting for transfers between devices  184 us
    reduce_scatter x1, waiting for transfers between devices, on_device(): lax.psum_scatter(jnp.concatenate([gate_up_part, down_part], axis=1), 'dp'...  166 us
    another operation x40, other arithmetic, delta_block(): lax.linalg.triangular_solve(coupling + jnp.eye(block_len, dtype=jnp.float...  162 us
    psum x2, waiting for transfers between devices, on_device(): small_sums = lax.psum(lax.psum(here_x, axis_name='tensor'), 'dp')  89 us
    dot_general x72, matrix products, exact_dot(): return jnp.dot(left, right, precision=highest)  82.1 us
    all_gather x1, waiting for transfers between devices, on_device(): lax.all_gather(mixer_joined, 'dp', axis=0, tiled=True)  52 us
    all_gather x1, waiting for transfers between devices, on_device(): lax.all_gather(ffn_joined, 'dp', axis=0, tiled=True)  50.1 us
    unnamed x254, local copies, waits for them, and re-layouts  41.7 us
  transfers between devices with their start and end apart: 12, of which 10 were waited for; matrix products, arithmetic and copies ran while one was open for 22% of the time, Pallas kernels for 0%

profile of v1, /device:TPU:8, one launch (start us, length us, event | category | flops | bytes accessed | tf_op | source)
XLA Modules:
  0.0 1230.3 jit_solution(15022270990851615085)
XLA Ops:
  14.0 8.7 all_gather.24
  23.0 52.0 %all-gather.5.cloned.1.call-done = bf16[1024,3080]{1,0:T(8,128)(2,1)} async-done(((bf16[64,3080]{1,0:T(8,128)(2,1)}), bf16[1024,3080]{1,0:T(8,128)(2,1)}) %all-gather.5.cloned.1.call-update) | async-done | bytes 6307856 | tf_op jit(solution)/shard_map/all_gather | solution.py:202
  75.0 5.6 fusion.229
  109.9 144.1 %while.98 = (s32[]{:T(128)}, f32[4,256,128]{2,1,0:T(8,128)S(1)}, f32[4,4,64,256]{3,1,2,0:T(4,128)}, f32[4,4,64,64]{3,2,1,0:T(8,128)}, f32[4,4,128,64]{2,3,1,0:T(...) while((s32[]{:T(128)}, f32[4,256,128]{2,1,0:T(8,128)S(1)}, ...), condition=%wide.region_5.6_spmd.clone.clone, body=%wide.region_3.5_spmd.clone.clone.sunk | while | flops 479990848 | bytes 12846126 | solution.py:100
  115.2 19.7 %custom-call.48 = f32[4,1,64,64]{2,3,1,0:T(8,128)S(1)} custom-call(f32[4,1,64,64]{3,2,1,0:T(8,128)S(1)} %add_bitcast_fusion.4), custom_call_target="InvertDiagBlocksLowerTriangular" | custom-call | tf_op jit(solution)/shard_map/jvp(vmap())/while/body/eval_jaxpr/triangular_solve | solution.py:70
  151.2 19.7 %custom-call.48 = f32[4,1,64,64]{2,3,1,0:T(8,128)S(1)} custom-call(f32[4,1,64,64]{3,2,1,0:T(8,128)S(1)} %add_bitcast_fusion.4), custom_call_target="InvertDiagBlocksLowerTriangular" | custom-call | tf_op jit(solution)/shard_map/jvp(vmap())/while/body/eval_jaxpr/triangular_solve | solution.py:70
  187.2 19.7 %custom-call.48 = f32[4,1,64,64]{2,3,1,0:T(8,128)S(1)} custom-call(f32[4,1,64,64]{3,2,1,0:T(8,128)S(1)} %add_bitcast_fusion.4), custom_call_target="InvertDiagBlocksLowerTriangular" | custom-call | tf_op jit(solution)/shard_map/jvp(vmap())/while/body/eval_jaxpr/triangular_solve | solution.py:70
  223.2 19.7 %custom-call.48 = f32[4,1,64,64]{2,3,1,0:T(8,128)S(1)} custom-call(f32[4,1,64,64]{3,2,1,0:T(8,128)S(1)} %add_bitcast_fusion.4), custom_call_target="InvertDiagBlocksLowerTriangular" | custom-call | tf_op jit(solution)/shard_map/jvp(vmap())/while/body/eval_jaxpr/triangular_solve | solution.py:70
  268.4 14.1 %all_gather.30 = bf16[256,1024]{1,0:T(8,128)(2,1)S(1)} all-gather(bf16[128,1024]{1,0:T(8,128)(2,1)S(1)} %copy-done.41), channel_id=1, replica_groups=mesh['dp'=16,'tensor'=2] {'tensor'}, dimensions={0}, use_global_device_ids=true | all-gather | bytes 786432 | tf_op jit(solution)/shard_map/all_gather | solution.py:246
  282.5 7.5 reduce-scatter.9.cloned.1.call-done
  291.3 8.8 all_gather.27
  300.2 50.1 %all-gather.9.cloned.1.call-done = bf16[1024,2816]{1,0:T(8,128)(2,1)} async-done(((bf16[64,2816]{1,0:T(8,128)(2,1)}), bf16[1024,2816]{1,0:T(8,128)(2,1)}) %all-gather.9.cloned.1.call-update) | async-done | bytes 5767184 | tf_op jit(solution)/shard_map/all_gather | solution.py:230
  350.3 5.9 fusion.231
  356.1 38.9 %all-gather.11.cloned.1.call-done = bf16[1024,1408]{1,0:T(8,128)(2,1)} async-done(((bf16[64,1408]{1,0:T(8,128)(2,1)}), bf16[1024,1408]{1,0:T(8,128)(2,1)}) %all-gather.11.cloned.1.call-update) | async-done | bytes 2883600 | tf_op jit(solution)/shard_map/all_gather | solution.py:231
  395.0 5.0 multiply_convert_fusion.1
  416.5 4.9 fusion.191
  424.9 15.0 %reduce-scatter.11.cloned.1.call-done = bf16[128,1024]{1,0:T(8,128)(2,1)} async-done(((bf16[256,1024]{1,0:T(8,128)(2,1)}), bf16[128,1024]{1,0:T(8,128)(2,1)}) %reduce-scatter.11.cloned.1.call-update) | async-done | bytes 262160 | tf_op jit(solution)/shard_map/reduce_scatter | solution.py:239
  442.3 8.5 all_gather.31
  465.3 191.6 %while.99 = (s32[]{:T(128)}, f32[4,256,128]{2,1,0:T(8,128)S(1)}, f32[4,4,64,128]{3,2,1,0:T(8,128)}, f32[4,4,64,128]{3,2,1,0:T(8,128)}, f32[4,4,64,256]{3,2,1,0:T...) while((s32[]{:T(128)}, f32[4,256,128]{2,1,0:T(8,128)S(1)}, ...), condition=%wide.region_24.25_spmd.clone.clone, body=%wide.region_13.24_spmd.clone.clone.sunk | while | flops 971683904 | bytes 18991880 | solution.py:100
  473.0 19.7 %custom-call.49 = f32[4,1,64,64]{2,3,1,0:T(8,128)S(1)} custom-call(f32[4,1,64,64]{3,2,1,0:T(8,128)S(1)} %add_bitcast_fusion.5), custom_call_target="InvertDiagBlocksLowerTriangular" | custom-call | tf_op jit(solution)/shard_map/transpose(jvp(vmap()))/while/body/eval_jaxpr/triangular_solve | solution.py:70
  520.8 19.7 %custom-call.49 = f32[4,1,64,64]{2,3,1,0:T(8,128)S(1)} custom-call(f32[4,1,64,64]{3,2,1,0:T(8,128)S(1)} %add_bitcast_fusion.5), custom_call_target="InvertDiagBlocksLowerTriangular" | custom-call | tf_op jit(solution)/shard_map/transpose(jvp(vmap()))/while/body/eval_jaxpr/triangular_solve | solution.py:70
  568.6 19.7 %custom-call.49 = f32[4,1,64,64]{2,3,1,0:T(8,128)S(1)} custom-call(f32[4,1,64,64]{3,2,1,0:T(8,128)S(1)} %add_bitcast_fusion.5), custom_call_target="InvertDiagBlocksLowerTriangular" | custom-call | tf_op jit(solution)/shard_map/transpose(jvp(vmap()))/while/body/eval_jaxpr/triangular_solve | solution.py:70
  616.4 19.7 %custom-call.49 = f32[4,1,64,64]{2,3,1,0:T(8,128)S(1)} custom-call(f32[4,1,64,64]{3,2,1,0:T(8,128)S(1)} %add_bitcast_fusion.5), custom_call_target="InvertDiagBlocksLowerTriangular" | custom-call | tf_op jit(solution)/shard_map/transpose(jvp(vmap()))/while/body/eval_jaxpr/triangular_solve | solution.py:70
  701.6 5.7 convolution_convert_fusion
  707.6 7.1 fusion.169
  715.2 6.9 reduce-scatter.15.cloned.1.call-done
  724.1 11.7 pad_maximum_fusion
  739.5 7.2 pad_maximum_fusion.1
  746.7 18.0 %copy.246 = f32[1024,4104]{1,0:T(8,128)} copy(f32[1024,4104]{0,1:T(8,128)} %pad_maximum_fusion.1) | data formatting | bytes 33619968
  766.9 166.2 %reduce-scatter.17.cloned.1.call-done = f32[64,4224]{1,0:T(8,128)} async-done(((f32[1024,4224]{1,0:T(8,128)}), f32[64,4224]{1,0:T(8,128)}) %reduce-scatter.17.cloned.1.call-update) | async-done | bytes 1081360 | tf_op jit(solution)/shard_map/reduce_scatter | solution.py:261
  935.3 183.0 %reduce-scatter.19.cloned.1.call-done = f32[64,4104]{1,0:T(8,128)} async-done(((f32[1024,4104]{1,0:T(8,128)}), f32[64,4104]{1,0:T(8,128)}) %reduce-scatter.19.cloned.1.call-update) | async-done | bytes 1050640
  1124.3 89.0 %all-reduce.38.cloned.1.call-done = (f32[1024]{0:T(1024)}, f32[4,1024]{1,0:T(4,128)}, f32[4,1024]{1,0:T(4,128)}, f32[4,2048]{1,0:T(4,128)}, f32[8]{0:T(128)}, /*index=5*/f32[8]{0:T(128)}, f32[256]{0:T(256)}, f32[1024]{0:T(1024)}) async-done(((f32[1024]{0:T(1024)}, f32[4,1024]{1,0:T(4,128)}, f32[4,1024]{1,0:T(4,128)}, f32[4,2048]{1,0:T(4,128)}, f32[8]{0:T(128)}, /*index=5*/f32[8]{0:T(128)}, f32[256]{0:T(256)}, ...) | async-done | bytes 74832 | tf_op jit(solution)/shard_map/psum | solution.py:304
  (704 shorter events, 335.2 us)
Async XLA Ops:
  7.2 67.8 %all-gather.5.cloned.1.call-start = ((), (), s32[]{:S(2)}) async-start(), calls=%async_computation.6 | async-start | bytes 6963200 | tf_op jit(solution)/shard_map/all_gather | solution.py:202
  10.8 251.8 %all-gather.7.cloned.1.call-start = ((), (), s32[]{:S(2)}) async-start(), calls=%async_computation.7 | async-start | bytes 2228224 | tf_op jit(solution)/shard_map/all_gather | solution.py:203
  11.5 278.4 %reduce-scatter.9.cloned.1.call-start = ((), (), s32[]{:S(2)}) async-start(), calls=%async_computation.8 | async-start | bytes 1572864 | tf_op jit(solution)/shard_map/reduce_scatter | solution.py:223
  12.9 67.7 %copy-start.104 = (f32[128]{0:T(128)}, f32[128]{0:T(128)S(1)}, u32[]{:S(2)}) copy-start(f32[128]{0:T(128)S(1)} %add_rsqrt_fusion.3) | copy-start | bytes 1540
  22.7 52.3 %copy-start.30 = (bf16[256,1024]{1,0:T(8,128)(2,1)}, bf16[256,1024]{1,0:T(8,128)(2,1)S(1)}, u32[]{:S(2)}) copy-start(bf16[256,1024]{1,0:T(8,128)(2,1)S(1)} %all_gather.24) | copy-start | bytes 1572868
  22.7 237.0 %copy-start.66 = (f32[1,2,4,128]{3,1,2,0:T(2,128)}, f32[1,2,4,128]{3,1,2,0:T(2,128)S(1)}, u32[]{:S(2)}) copy-start(f32[1,2,4,128]{3,1,2,0:T(2,128)S(1)} %copy.322) | copy-start | bytes 12292
  22.7 62.9 %copy-start.110 = (f32[4]{0:T(128)}, f32[4]{0:T(128)S(1)}, u32[]{:S(2)}) copy-start(f32[4]{0:T(128)S(1)} %exponential_negate_fusion) | copy-start | bytes 52
  22.8 63.1 %copy-start.84 = (f32[1,512]{1,0:T(1,128)}, f32[1,512]{1,0:T(1,128)S(1)}, u32[]{:S(2)}) copy-start(f32[1,512]{1,0:T(1,128)S(1)} %get-tuple-element.2640) | copy-start | bytes 6148
  22.8 63.1 %copy-start.88 = (f32[1,512]{1,0:T(1,128)}, f32[1,512]{1,0:T(1,128)S(1)}, u32[]{:S(2)}) copy-start(f32[1,512]{1,0:T(1,128)S(1)} %get-tuple-element.2641) | copy-start | bytes 6148
  22.8 63.1 %copy-start.92 = (f32[1,512]{1,0:T(1,128)}, f32[1,512]{1,0:T(1,128)S(1)}, u32[]{:S(2)}) copy-start(f32[1,512]{1,0:T(1,128)S(1)} %get-tuple-element.2639) | copy-start | bytes 6148
  22.8 63.1 %copy-start.96 = (f32[1,512]{1,0:T(1,128)}, f32[1,512]{1,0:T(1,128)S(1)}, u32[]{:S(2)}) copy-start(f32[1,512]{1,0:T(1,128)S(1)} %get-tuple-element.2638) | copy-start | bytes 6148
  22.8 63.1 %copy-start.82 = (f32[1,512]{1,0:T(1,128)}, f32[1,512]{1,0:T(1,128)S(1)}, u32[]{:S(2)}) copy-start(f32[1,512]{1,0:T(1,128)S(1)} %get-tuple-element.2644) | copy-start | bytes 6148
  22.9 63.1 %copy-start.86 = (f32[1,512]{1,0:T(1,128)}, f32[1,512]{1,0:T(1,128)S(1)}, u32[]{:S(2)}) copy-start(f32[1,512]{1,0:T(1,128)S(1)} %get-tuple-element.2645) | copy-start | bytes 6148
  22.9 63.1 %copy-start.90 = (f32[1,512]{1,0:T(1,128)}, f32[1,512]{1,0:T(1,128)S(1)}, u32[]{:S(2)}) copy-start(f32[1,512]{1,0:T(1,128)S(1)} %get-tuple-element.2643) | copy-start | bytes 6148
  22.9 63.1 %copy-start.94 = (f32[1,512]{1,0:T(1,128)}, f32[1,512]{1,0:T(1,128)S(1)}, u32[]{:S(2)}) copy-start(f32[1,512]{1,0:T(1,128)S(1)} %get-tuple-element.2642) | copy-start | bytes 6148
  22.9 72.6 %copy-start.68 = (f32[1,1024]{1,0:T(1,128)}, f32[1,1024]{1,0:T(1,128)S(1)}, u32[]{:S(2)}) copy-start(f32[1,1024]{1,0:T(1,128)S(1)} %get-tuple-element.2636) | copy-start | bytes 12292
  22.9 72.6 %copy-start.70 = (f32[1,1024]{1,0:T(1,128)}, f32[1,1024]{1,0:T(1,128)S(1)}, u32[]{:S(2)}) copy-start(f32[1,1024]{1,0:T(1,128)S(1)} %get-tuple-element.2637) | copy-start | bytes 12292
  22.9 72.6 %copy-start.72 = (f32[1,1024]{1,0:T(1,128)}, f32[1,1024]{1,0:T(1,128)S(1)}, u32[]{:S(2)}) copy-start(f32[1,1024]{1,0:T(1,128)S(1)} %get-tuple-element.2635) | copy-start | bytes 12292
  22.9 72.6 %copy-start.80 = (f32[1,1024]{1,0:T(1,128)}, f32[1,1024]{1,0:T(1,128)S(1)}, u32[]{:S(2)}) copy-start(f32[1,1024]{1,0:T(1,128)S(1)} %get-tuple-element.2634) | copy-start | bytes 12292
  266.2 84.0 %all-gather.9.cloned.1.call-start = ((), (), s32[]{:S(2)}) async-start(), calls=%async_computation.9 | async-start | bytes 6127616 | tf_op jit(solution)/shard_map/all_gather | solution.py:230
  267.1 127.9 %all-gather.11.cloned.1.call-start = ((), (), s32[]{:S(2)}) async-start(), calls=%async_computation.10 | async-start | bytes 3063808 | tf_op jit(solution)/shard_map/all_gather | solution.py:231
  267.7 155.3 %reduce-scatter.13.cloned.1.call-start = ((), (), s32[]{:S(2)}) async-start(), calls=%async_computation.12 | async-start | bytes 1572864 | tf_op jit(solution)/shard_map/reduce_scatter | solution.py:254
  268.4 126.6 %copy-start.112 = (bf16[256]{0:T(256)(128)(2,1)}, bf16[256]{0:T(256)(128)(2,1)S(1)}, u32[]{:S(2)}) copy-start(bf16[256]{0:T(256)(128)(2,1)S(1)} %compare_convert_fusion) | copy-start | bytes 1540
  282.5 112.5 %copy-start.29 = (bf16[256,1024]{1,0:T(8,128)(2,1)}, bf16[256,1024]{1,0:T(8,128)(2,1)S(1)}, u32[]{:S(2)}) copy-start(bf16[256,1024]{1,0:T(8,128)(2,1)S(1)} %all_gather.30) | copy-start | bytes 1572868
  291.2 64.9 %copy-start.106 = (f32[128]{0:T(128)}, f32[128]{0:T(128)S(1)}, u32[]{:S(2)}) copy-start(f32[128]{0:T(128)S(1)} %add_rsqrt_fusion.2) | copy-start | bytes 1540
  300.2 56.0 %copy-start.32 = (bf16[256,1024]{1,0:T(8,128)(2,1)}, bf16[256,1024]{1,0:T(8,128)(2,1)S(1)}, u32[]{:S(2)}) copy-start(bf16[256,1024]{1,0:T(8,128)(2,1)S(1)} %all_gather.27) | copy-start | bytes 1572868
  403.8 36.1 %reduce-scatter.11.cloned.1.call-start = ((), (), s32[]{:S(2)}) async-start(), calls=%async_computation.11 | async-start | bytes 786432 | tf_op jit(solution)/shard_map/reduce_scatter | solution.py:239
  407.8 314.4 %reduce-scatter.15.cloned.1.call-start = ((), (), s32[]{:S(2)}) async-start(), calls=%async_computation.13 | async-start | bytes 786432 | tf_op jit(solution)/shard_map/reduce_scatter | solution.py:270
  707.4 59.4 %all-reduce.40.cloned.1.call-start = ((), (), s32[]{:S(2)}) async-start(), calls=%async_computation.17 | async-start | bytes 151552 | tf_op jit(solution)/shard_map/psum | solution.py:304
  724.0 209.0 %reduce-scatter.17.cloned.1.call-start = ((), (), s32[]{:S(2)}) async-start(), calls=%async_computation.14 | async-start | bytes 18382848 | tf_op jit(solution)/shard_map/reduce_scatter | solution.py:261
  735.8 382.5 %reduce-scatter.19.cloned.1.call-start = ((), (), s32[]{:S(2)}) async-start(), calls=%async_computation.15 | async-start | bytes 18382848
  764.7 448.5 %all-reduce.38.cloned.1.call-start = ((), (), s32[]{:S(2)}) async-start(), calls=%async_computation.16 | async-start | bytes 151552 | tf_op jit(solution)/shard_map/psum | solution.py:304
  (102 other events, 610.1 us)
Sparse Core Ops, SparseCore 0:
  10.9 64.0 all-gather.4
  77.2 39.0 all-gather.6
  266.3 23.5 reduce-scatter.8
  292.7 57.5 all-gather.8
  352.4 42.5 all-gather.10
  403.9 18.9 reduce-scatter.12
  425.2 14.6 reduce-scatter.10
  707.5 14.6 reduce-scatter.14
  726.5 21.5 all-reduce.39
  752.1 180.9 reduce-scatter.16
  937.2 181.0 reduce-scatter.18
  1122.6 90.5 all-reduce.37
